TPU v7x, 512 devices: a whole 4x8x8 slice. The times are simulated.
512 devices in a mesh: phase: 8 (over x, core), expert: 64 (over y, z).
Axes of the slice: x: 4, y: 8, z: 8, core: 2. Of those that a mesh axis runs over, the one named last changes fastest.
Arguments:
- fwd_acts: bfloat16 [8, 8192, 2048], P('phase', 'expert'), may hold values from -6 to 6
- fwd_routes: int32 [8, 8192, 1], P('phase', 'expert'), may hold values from 0 to 7; in each aligned block of 128 rows (0 to 127, 128 to 255, ..., all dimensions but the last counted through in order) at most 18 rows name the same one
- fwd_weights: float32 [8, 8192, 1], P('phase', 'expert'), may hold values from 0.1 to 1
- fwd_lengths: int32 [8, 16], P('phase'), may hold values from 1 to 2048, 8192 in all within a row
- fwd_tenants: int32 [8, 16], P('phase'), may hold values from 0 to 1
- bwd_acts: bfloat16 [8, 8192, 2048], P('phase', 'expert'), may hold values from -6 to 6
- bwd_routes: int32 [8, 8192, 1], P('phase', 'expert'), may hold values from 0 to 7; in each aligned block of 128 rows (0 to 127, 128 to 255, ..., all dimensions but the last counted through in order) at most 18 rows name the same one
- bwd_weights: float32 [8, 8192, 1], P('phase', 'expert'), may hold values from 0.1 to 1
- bwd_lengths: int32 [8, 16], P('phase'), may hold values from 1 to 2048, 8192 in all within a row
- bwd_tenants: int32 [8, 16], P('phase'), may hold values from 0 to 1
- bwd_cotangent: bfloat16 [8, 8192, 2048], P('phase', 'expert'), may hold values from -6 to 6
- prompts: bfloat16 [8, 2, 10, 2048], P('phase'), may hold values from -6 to 6
- norm_gain: float32 [8, 2048], P('phase'), may hold values from 0.1 to 1.9
- w_gate: bfloat16 [8, 64, 2048, 128], P('phase', 'expert'), may hold values from -0.125 to 0.125
- w_up: bfloat16 [8, 64, 2048, 128], P('phase', 'expert'), may hold values from -0.125 to 0.125
- w_down: bfloat16 [8, 64, 128, 2048], P('phase', 'expert'), may hold values from -0.1875 to 0.1875
Outputs:
- next_acts: bfloat16 [8, 8192, 2048], P('phase', 'expert')
- prev_grads: bfloat16 [8, 8192, 2048], P('phase', 'expert')
- prompt_grads: bfloat16 [8, 2, 10, 2048], P('phase')
Inputs may be any that keep to these rules, and one draw needn't show every extreme that they name: `fwd_routes`: each row names 1 different experts; among the 128 tokens of one device no expert is named by more than 18 rows, a bound that some block reaches. `bwd_routes`: each row names 1 different experts; among the 128 tokens of one device no expert is named by more than 18 rows, a bound that some block reaches.
All inputs are finite; a program needn't handle non-finite values.
Results may differ from a plain program's by a relative error of at most 0.008.
Values may be sent and summed in bfloat16 or wider, within the bound.
No kernel may reach another device: no remote copies, remote signals or barrier semaphores. Data moves between devices by JAX's collectives and lax.ppermute only.
A program may use at most 128 MiB of HBM per device.

v0:
```python
import jax
import jax.numpy as jnp
from jax import lax
from jax.sharding import PartitionSpec as P

EXPERTS = 8
TENANTS = 2
PLEN = 10
CAP = 18
EPS = 1e-06


def shifted(block, axis, distance):
    devices = range(lax.axis_size(axis))
    route = [(i - distance, i) for i in devices if i - distance in devices]
    return lax.ppermute(block, axis, route)


def token_layout(lengths, tenants, tok_count):
    first_row = lax.axis_index("expert") * tok_count
    token_index = first_row + jnp.arange(tok_count, dtype=jnp.int32)
    seg_ends = jnp.cumsum(lengths)
    seg_starts = seg_ends - lengths
    member = (seg_starts[None, :] <= token_index[:, None]).astype(jnp.int32)
    segment = jnp.sum(member, axis=1) - 1
    chosen = (jnp.arange(lengths.shape[0], dtype=jnp.int32)[None, :] == segment[:, None]).astype(
        jnp.int32
    )
    position = token_index - jnp.sum(chosen * seg_starts[None, :], axis=1)
    tenant = jnp.sum(chosen * tenants[None, :], axis=1)
    return (position, tenant)


def prepare(acts, lengths, tenants, prompt_table, gain_row):
    tok_count = acts.shape[0]
    position, tenant = token_layout(lengths, tenants, tok_count)
    prompt_slot = position < PLEN
    flat_index = tenant * PLEN + jnp.minimum(position, PLEN - 1)
    selector = (
        flat_index[:, None] == jnp.arange(TENANTS * PLEN, dtype=jnp.int32)[None, :]
    ) & prompt_slot[:, None]
    flat_table = prompt_table.reshape(TENANTS * PLEN, prompt_table.shape[-1])
    prompt_rows = jnp.dot(
        selector.astype(jnp.bfloat16), flat_table, preferred_element_type=jnp.float32
    ).astype(jnp.bfloat16)
    inputs = jnp.where(prompt_slot[:, None], prompt_rows, acts)
    widened = inputs.astype(jnp.float32)
    inv_scale = lax.rsqrt(jnp.mean(widened * widened, axis=1, keepdims=True) + EPS)
    normed = (widened * inv_scale * gain_row[None, :]).astype(jnp.bfloat16)
    return (selector, widened, inv_scale, normed, prompt_slot)


def routing(routes, weights):
    tok_count, top_count = routes.shape
    flattened = routes.reshape(tok_count * top_count)
    onehot = (flattened[:, None] == jnp.arange(EXPERTS, dtype=jnp.int32)[None, :]).astype(jnp.int32)
    ranking = jnp.sum((jnp.cumsum(onehot, axis=0) - 1) * onehot, axis=1)
    target = (flattened * CAP + ranking).reshape(tok_count, top_count)
    matches = target[:, :, None] == jnp.arange(EXPERTS * CAP, dtype=jnp.int32)[None, None, :]
    picker = jnp.transpose(jnp.any(matches, axis=1).astype(jnp.bfloat16))
    mixing = jnp.sum(jnp.where(matches, weights[:, :, None], 0.0), axis=1)
    return (picker, mixing)


def dispatch(picker, sources):
    shards = lax.axis_size("expert") // EXPERTS
    stacked, tok_count, model_width = sources.shape
    packed = jnp.einsum("qn,mnd->mqd", picker, sources, preferred_element_type=jnp.float32).astype(
        jnp.bfloat16
    )
    packed = jnp.broadcast_to(
        packed.reshape(stacked, 1, EXPERTS * CAP, model_width),
        (stacked, shards, EXPERTS * CAP, model_width),
    )
    packed = packed.reshape(stacked, shards * EXPERTS, CAP, model_width)
    received = lax.all_to_all(packed, "expert", split_axis=1, concat_axis=1, tiled=True)
    return received


def give_back(partial_value):
    shards = lax.axis_size("expert") // EXPERTS
    returned = lax.all_to_all(partial_value, "expert", split_axis=0, concat_axis=0, tiled=True)
    return jnp.sum(
        returned.reshape(shards, EXPERTS * CAP, partial_value.shape[-1]).astype(jnp.float32), axis=0
    )


def expert_forward(slot_rows, gate_weight, up_weight, down_weight):
    gate_pre = jnp.dot(slot_rows, gate_weight, preferred_element_type=jnp.float32)
    upper = jnp.dot(slot_rows, up_weight, preferred_element_type=jnp.float32)
    hidden = (jax.nn.silu(gate_pre) * upper).astype(jnp.bfloat16)
    return jnp.dot(hidden, down_weight, preferred_element_type=jnp.float32).astype(jnp.bfloat16)


def expert_backward(slot_rows, slot_grads, gate_weight, up_weight, down_weight):
    gate_pre = jnp.dot(slot_rows, gate_weight, preferred_element_type=jnp.float32)
    upper = jnp.dot(slot_rows, up_weight, preferred_element_type=jnp.float32)
    contract = (((1,), (1,)), ((), ()))
    hidden_grad = lax.dot_general(
        slot_grads, down_weight, contract, preferred_element_type=jnp.float32
    )
    sigmoid_gate = jax.nn.sigmoid(gate_pre)
    gate_grad = (
        hidden_grad * upper * sigmoid_gate * (1.0 + gate_pre * (1.0 - sigmoid_gate))
    ).astype(jnp.bfloat16)
    up_grad = (hidden_grad * (gate_pre * sigmoid_gate)).astype(jnp.bfloat16)
    back_rows = lax.dot_general(
        gate_grad, gate_weight, contract, preferred_element_type=jnp.float32
    )
    back_rows = back_rows + lax.dot_general(
        up_grad, up_weight, contract, preferred_element_type=jnp.float32
    )
    return back_rows.astype(jnp.bfloat16)


def on_device(
    fwd_acts,
    fwd_routes,
    fwd_weights,
    fwd_lengths,
    fwd_tenants,
    bwd_acts,
    bwd_routes,
    bwd_weights,
    bwd_lengths,
    bwd_tenants,
    bwd_cotangent,
    prompts,
    norm_gain,
    w_gate,
    w_up,
    w_down,
):
    gate_weight = w_gate[0, 0]
    up_weight = w_up[0, 0]
    down_weight = w_down[0, 0]
    gain_row = norm_gain[0]
    prompt_table = prompts[0]
    model_width = fwd_acts.shape[-1]
    fwd_select, fwd_wide, fwd_scale, fwd_normed, fwd_slot = prepare(
        fwd_acts[0], fwd_lengths[0], fwd_tenants[0], prompt_table, gain_row
    )
    fwd_picker, fwd_mixing = routing(fwd_routes[0], fwd_weights[0])
    arrived = dispatch(fwd_picker, fwd_normed[None])
    senders = arrived.shape[1]
    partial_value = expert_forward(
        arrived[0].reshape(senders * CAP, model_width), gate_weight, up_weight, down_weight
    )
    summed = give_back(partial_value.reshape(senders, CAP, model_width))
    mixed_out = fwd_wide + jnp.dot(fwd_mixing, summed, precision=lax.Precision.HIGHEST)
    leaving = mixed_out.astype(jnp.bfloat16)
    next_acts = shifted(leaving, "phase", 1)
    bwd_select, bwd_wide, bwd_scale, bwd_normed, bwd_slot = prepare(
        bwd_acts[0], bwd_lengths[0], bwd_tenants[0], prompt_table, gain_row
    )
    bwd_picker, bwd_mixing = routing(bwd_routes[0], bwd_weights[0])
    cotangent = bwd_cotangent[0]
    arrived_back = dispatch(bwd_picker, jnp.stack([bwd_normed, cotangent]))
    partial_back = expert_backward(
        arrived_back[0].reshape(senders * CAP, model_width),
        arrived_back[1].reshape(senders * CAP, model_width),
        gate_weight,
        up_weight,
        down_weight,
    )
    summed_back = give_back(partial_back.reshape(senders, CAP, model_width))
    normed_grad = jnp.dot(bwd_mixing, summed_back, precision=lax.Precision.HIGHEST)
    scaled = normed_grad * gain_row[None, :]
    inner = jnp.mean(bwd_wide * scaled, axis=1, keepdims=True)
    input_grad = (
        cotangent.astype(jnp.float32) + bwd_scale * scaled - bwd_wide * bwd_scale**3 * inner
    )
    to_prev = jnp.where(bwd_slot[:, None], 0.0, input_grad).astype(jnp.bfloat16)
    prev_grads = shifted(to_prev, "phase", -1)
    local_sums = jnp.dot(
        jnp.transpose(bwd_select.astype(jnp.float32)), input_grad, precision=lax.Precision.HIGHEST
    )
    totals = lax.psum(local_sums, "expert")
    prompt_grads = totals.reshape(1, TENANTS, PLEN, model_width).astype(jnp.bfloat16)
    return (next_acts[None], prev_grads[None], prompt_grads)


def solution(mesh):
    placed = (
        P("phase", "expert", None),
        P("phase", "expert", None),
        P("phase", "expert", None),
        P("phase", None),
        P("phase", None),
        P("phase", "expert", None),
        P("phase", "expert", None),
        P("phase", "expert", None),
        P("phase", None),
        P("phase", None),
        P("phase", "expert", None),
        P("phase", None, None, None),
        P("phase", None),
        P("phase", "expert", None, None),
        P("phase", "expert", None, None),
        P("phase", "expert", None, None),
    )
    return jax.shard_map(
        on_device,
        mesh=mesh,
        in_specs=placed,
        out_specs=(
            P("phase", "expert", None),
            P("phase", "expert", None),
            P("phase", None, None, None),
        ),
        check_vma=False,
    )
```

profile of v0, /device:TPU:36, one launch (start us, length us, event | category | flops | bytes accessed | tf_op | source)
XLA Modules:
  0.0 1311.5 jit_solution(975837895841320012)
XLA Ops:
  0.6 0.0 copy-start
  0.7 0.9 reduce-window_1_clone.1
  1.6 0.7 subtract_bitcast_fusion
  2.2 0.8 reduce-window_clone.1
  3.1 0.7 subtract_bitcast_fusion.1
  3.7 0.9 copy.27
  4.7 0.1 convert_reduce_fusion
  4.8 0.7 select_reduce_fusion.4
  5.5 1.5 multiply_reduce_fusion.2
  7.0 0.7 fusion.49
  7.8 0.2 reduce_window_sum.26
  7.9 0.8 select_reduce_fusion.1
  8.8 0.7 multiply_add_fusion.1
  9.4 1.1 fusion.7
  10.5 2.7 broadcast_in_dim.97
  13.3 7.6 broadcast_in_dim.98
  20.8 16.6 %all-to-all-start = ((bf16[1,64,18,2048]{3,2,0,1:T(8,128)(2,1)}), bf16[1,64,18,2048]{3,2,0,1:T(8,128)(2,1)}, u32[]{:S(2)}, u32[]{:S(2)}) async-start(bf16[1,64,18,2048]{3,2,0,1:T(8,128)(2,1)} %bitcast.72), calls=%async_computation | async-start | bytes 12582912 | tf_op jit(solution)/shard_map/all_to_all | solution.py:76
  37.5 0.1 fusion.48
  37.6 0.2 reduce_window_sum.27
  37.8 0.0 copy-done.10
  37.8 0.1 select_reduce_fusion.2
  37.8 0.2 select_reduce_fusion
  38.0 1.5 multiply_reduce_fusion.1
  39.6 0.2 fusion.25
  39.7 0.5 fusion.3
  40.2 2.3 copy.29
  42.5 214.9 %all-to-all-done = bf16[1,64,18,2048]{3,2,0,1:T(8,128)(2,1)} async-done(((bf16[1,64,18,2048]{3,2,0,1:T(8,128)(2,1)}), bf16[1,64,18,2048]{3,2,0,1:T(8,128)(2,1)}, u32[]{:S(2)}, u32[]{:S(2)}) %all-to-all-start) | async-done | bytes 4718624 | tf_op jit(solution)/shard_map/all_to_all | solution.py:76
  257.4 8.3 broadcast_in_dim.104
  265.7 20.2 %all-to-all-start.2 = ((bf16[2,64,18,2048]{3,0,2,1:T(2,128)(2,1)}), bf16[2,64,18,2048]{3,0,2,1:T(2,128)(2,1)}, u32[]{:S(2)}, u32[]{:S(2)}) async-start(bf16[2,64,18,2048]{3,0,2,1:T(2,128)(2,1)} %bitcast.71), calls=%async_computation.2 | async-start | bytes 18874368 | tf_op jit(solution)/shard_map/all_to_all | solution.py:76
  285.9 0.0 copy-start.2
  285.9 7.8 reshape_squeeze.21
  293.8 4.6 fusion.37
  298.3 9.6 convolution_convert_fusion
  307.9 7.6 reshape.228
  315.5 246.5 %all-to-all-done.2 = bf16[2,64,18,2048]{3,0,2,1:T(2,128)(2,1)} async-done(((bf16[2,64,18,2048]{3,0,2,1:T(2,128)(2,1)}), bf16[2,64,18,2048]{3,0,2,1:T(2,128)(2,1)}, u32[]{:S(2)}, u32[]{:S(2)}) %all-to-all-start.2) | async-done | bytes 9437216 | tf_op jit(solution)/shard_map/all_to_all | solution.py:76
  562.0 44.8 %all-to-all-start.1 = ((bf16[64,18,2048]{2,1,0:T(8,128)(2,1)}), bf16[64,18,2048]{2,1,0:T(8,128)(2,1)}, u32[]{:S(2)}, u32[]{:S(2)}) async-start(bf16[64,18,2048]{2,1,0:T(8,128)(2,1)} %reshape.228), calls=%async_computation.1 | async-start | bytes 12582912 | tf_op jit(solution)/shard_map/all_to_all | solution.py:82
  606.8 48.0 %slice_reduce_fusion = (bf16[64,18,2048]{2,1,0:T(8,128)(2,1)}, bf16[64,18,2048]{2,1,0:T(8,128)(2,1)}) fusion(bf16[2,64,18,2048]{3,0,2,1:T(2,128)(2,1)} %all-to-all-done.2), kind=kLoop, calls=%fused_computation.1 | loop fusion | bytes 18874368 | tf_op jit(solution)/shard_map/slice | solution.py:160
  654.8 7.7 reshape_squeeze.23
  662.6 7.7 reshape_squeeze.24
  670.3 4.0 fusion.26
  674.3 0.0 copy-done.3
  674.3 2.2 fusion.35
  676.5 11.1 fusion.12
  687.6 7.5 fusion
  695.2 7.6 reshape.230
  702.8 99.0 %all-to-all-done.1 = bf16[64,18,2048]{2,1,0:T(8,128)(2,1)} async-done(((bf16[64,18,2048]{2,1,0:T(8,128)(2,1)}), bf16[64,18,2048]{2,1,0:T(8,128)(2,1)}, u32[]{:S(2)}, u32[]{:S(2)}) %all-to-all-start.1) | async-done | bytes 4718624 | tf_op jit(solution)/shard_map/all_to_all | solution.py:82
  801.8 16.9 %all-to-all-start.3 = ((bf16[64,18,2048]{2,1,0:T(8,128)(2,1)}), bf16[64,18,2048]{2,1,0:T(8,128)(2,1)}, u32[]{:S(2)}, u32[]{:S(2)}) async-start(bf16[64,18,2048]{2,1,0:T(8,128)(2,1)} %reshape.230), calls=%async_computation.3 | async-start | bytes 12582912 | tf_op jit(solution)/shard_map/all_to_all | solution.py:82
  818.7 8.5 reshape.231
  827.3 5.8 reduce_sum.130
  833.0 3.1 fusion.4
  836.2 1.9 collective-permute-start
  838.1 175.9 %all-to-all-done.3 = bf16[64,18,2048]{2,1,0:T(8,128)(2,1)} async-done(((bf16[64,18,2048]{2,1,0:T(8,128)(2,1)}), bf16[64,18,2048]{2,1,0:T(8,128)(2,1)}, u32[]{:S(2)}, u32[]{:S(2)}) %all-to-all-start.3) | async-done | bytes 4718624 | tf_op jit(solution)/shard_map/all_to_all | solution.py:82
  1014.0 8.6 reshape.233
  1022.5 4.7 reduce_sum.136
  1027.3 1.2 multiply_reduce_fusion
  1028.5 0.4 select_convert_fusion
  1028.9 1.9 collective-permute-start.1
  1030.8 0.0 collective-permute-done
  1030.8 0.5 fusion.53
  1031.3 276.7 %all-reduce.1 = bf16[20,2048]{1,0:T(8,128)(2,1)S(1)} all-reduce(f32[20,2048]{1,0:T(8,128)S(1)} %fusion.53), channel_id=1, replica_groups=mesh['phase'=8,'expert'=64] {'expert'}, use_global_device_ids=true, to_apply=%region_17.18 | all-reduce | flops 40960 | bytes 245760 | tf_op jit(solution)/shard_map/psum | solution.py:178
  1308.1 0.7 copy.30
  1308.8 0.0 collective-permute-done.1
  1308.8 1.9 copy.37
  1310.7 0.8 copy.38
  (30 shorter events, 0.2 us)
Async XLA Ops:
  0.6 297.7 %copy-start = (bf16[1,1,2048,128]{3,2,1,0:T(8,128)(2,1)S(1)}, bf16[1,1,2048,128]{3,2,1,0:T(8,128)(2,1)}, u32[]{:S(2)}) copy-start(bf16[1,1,2048,128]{3,2,1,0:T(8,128)(2,1)} %param.30) | copy-start | bytes 1572868
  20.8 16.7 %copy-start.7 = (s32[1,128,1]{1,2,0:T(1,128)S(1)}, s32[1,128,1]{1,2,0:T(1,128)}, u32[]{:S(2)}) copy-start(s32[1,128,1]{1,2,0:T(1,128)} %param.22) | copy-start | bytes 1540
  20.8 16.9 %copy-start.10 = (s32[1,16]{1,0:T(1,128)S(1)}, s32[1,16]{1,0:T(1,128)}, u32[]{:S(2)}) copy-start(s32[1,16]{1,0:T(1,128)} %param.25) | copy-start | bytes 196
  20.8 18.7 %copy-start.6 = (f32[1,2048]{1,0:T(1,128)S(1)}, f32[1,2048]{1,0:T(1,128)}, u32[]{:S(2)}) copy-start(f32[1,2048]{1,0:T(1,128)} %param.28) | copy-start | bytes 24580
  20.8 18.9 %copy-start.4 = (bf16[1,128,2048]{2,1,0:T(8,128)(2,1)S(1)}, bf16[1,128,2048]{2,1,0:T(8,128)(2,1)}, u32[]{:S(2)}) copy-start(bf16[1,128,2048]{2,1,0:T(8,128)(2,1)} %param.26) | copy-start | bytes 1572868
  20.8 236.6 %all-to-all-start = ((bf16[1,64,18,2048]{3,2,0,1:T(8,128)(2,1)}), bf16[1,64,18,2048]{3,2,0,1:T(8,128)(2,1)}, u32[]{:S(2)}, u32[]{:S(2)}) async-start(bf16[1,64,18,2048]{3,2,0,1:T(8,128)(2,1)} %bitcast.72), calls=%async_computation | async-start | bytes 12582912 | tf_op jit(solution)/shard_map/all_to_all | solution.py:76
  265.7 296.3 %all-to-all-start.2 = ((bf16[2,64,18,2048]{3,0,2,1:T(2,128)(2,1)}), bf16[2,64,18,2048]{3,0,2,1:T(2,128)(2,1)}, u32[]{:S(2)}, u32[]{:S(2)}) async-start(bf16[2,64,18,2048]{3,0,2,1:T(2,128)(2,1)} %bitcast.71), calls=%async_computation.2 | async-start | bytes 18874368 | tf_op jit(solution)/shard_map/all_to_all | solution.py:76
  285.9 7.8 copy-start.2
  562.0 239.8 %all-to-all-start.1 = ((bf16[64,18,2048]{2,1,0:T(8,128)(2,1)}), bf16[64,18,2048]{2,1,0:T(8,128)(2,1)}, u32[]{:S(2)}, u32[]{:S(2)}) async-start(bf16[64,18,2048]{2,1,0:T(8,128)(2,1)} %reshape.228), calls=%async_computation.1 | async-start | bytes 12582912 | tf_op jit(solution)/shard_map/all_to_all | solution.py:82
  670.2 4.0 copy-start.1
  670.3 4.0 copy-start.3
  801.8 212.2 %all-to-all-start.3 = ((bf16[64,18,2048]{2,1,0:T(8,128)(2,1)}), bf16[64,18,2048]{2,1,0:T(8,128)(2,1)}, u32[]{:S(2)}, u32[]{:S(2)}) async-start(bf16[64,18,2048]{2,1,0:T(8,128)(2,1)} %reshape.230), calls=%async_computation.3 | async-start | bytes 12582912 | tf_op jit(solution)/shard_map/all_to_all | solution.py:82
  827.3 5.8 copy-start.8
  836.2 194.6 %collective-permute-start = (bf16[128,2048]{1,0:T(8,128)(2,1)}, bf16[128,2048]{1,0:T(8,128)(2,1)}, u32[]{:S(2)}, u32[]{:S(2)}) collective-permute-start(bf16[128,2048]{1,0:T(8,128)(2,1)} %fusion.4), channel_id=1, source_target_pairs={{0,64},{64,128},{128,192},{192,256},{256,320},{320,384},{384,448},... | collective-permute-start | bytes 1572872 | tf_op jit(solution)/shard_map/ppermute | solution.py:16
  1022.5 4.7 copy-start.9
  1022.5 6.0 copy-start.5
  1028.9 279.9 %collective-permute-start.1 = (bf16[128,2048]{1,0:T(8,128)(2,1)S(1)}, bf16[128,2048]{1,0:T(8,128)(2,1)S(1)}, u32[]{:S(2)}, u32[]{:S(2)}) collective-permute-start(bf16[128,2048]{1,0:T(8,128)(2,1)S(1)} %get-tuple-element.23), channel_id=1, source_target_pairs={{64,0},{128,64},{192,128},{256,192},{320,256},{384,320},{448,384},... | collective-permute-start | bytes 1572872 | tf_op jit(solution)/shard_map/ppermute | solution.py:16
where the time goes:
time: 1310 us
  waiting for transfers between devices  736 us (56%)
  blocking collectives  277 us (21%)
  local copies, waits for them, and re-layouts  129 us (10%)
  starting transfers between devices  102 us (8%)
  matrix products  48.4 us (4%)
  other arithmetic  17.9 us (1%)
    all_to_all x2, waiting for transfers between devices, dispatch(): lax.all_to_all(packed, 'expert', split_axis=1, concat_axis=1, tiled=True)  461 us
    psum x1, blocking collectives, on_device(): totals = lax.psum(local_sums, 'expert')  277 us
    all_to_all x2, waiting for transfers between devices, give_back(): lax.all_to_all(partial_value, 'expert', split_axis=0, concat_axis=0, tile...  275 us
    all_to_all x2, starting transfers between devices, give_back(): lax.all_to_all(partial_value, 'expert', split_axis=0, concat_axis=0, tile...  61.7 us
    slice x1, local copies, waits for them, and re-layouts, on_device(): arrived_back[0].reshape(senders * CAP, model_width)  48 us
    all_to_all x2, starting transfers between devices, dispatch(): lax.all_to_all(packed, 'expert', split_axis=1, concat_axis=1, tiled=True)  36.9 us
  transfers between devices with their start and end apart: 6, of which 4 were waited for; matrix products, arithmetic and copies ran while one was open for 13% of the time, Pallas kernels for 0%

commit v1 on v0

--- a/solution.py
+++ b/solution.py
@@ -175,7 +175,8 @@
     local_sums = jnp.dot(
         jnp.transpose(bwd_select.astype(jnp.float32)), input_grad, precision=lax.Precision.HIGHEST
     )
-    totals = lax.psum(local_sums, "expert")
+    terms = lax.all_gather(local_sums, "expert", axis=0, tiled=False)
+    totals = terms.sum(axis=0)
     prompt_grads = totals.reshape(1, TENANTS, PLEN, model_width).astype(jnp.bfloat16)
     return (next_acts[None], prev_grads[None], prompt_grads)
 

time: 1310 us -> 1070 us (0.82)
  the two profiles are of different devices: /device:TPU:36 before, /device:TPU:27 now
where the time goes in v1:
time: 1070 us
  blocking collectives  619 us (58%)
  waiting for transfers between devices  201 us (19%)
  local copies, waits for them, and re-layouts  130 us (12%)
  matrix products  47.5 us (4%)
  starting transfers between devices  28.1 us (3%)
  other arithmetic  26.8 us (3%)
  between operations  14.3 us (1%)
    all_to_all x2, blocking collectives, dispatch(): lax.all_to_all(packed, 'expert', split_axis=1, concat_axis=1, tiled=True)  433 us
    all_to_all x1, waiting for transfers between devices, give_back(): lax.all_to_all(partial_value, 'expert', split_axis=0, concat_axis=0, tile...  192 us
    all_to_all x1, blocking collectives, give_back(): lax.all_to_all(partial_value, 'expert', split_axis=0, concat_axis=0, tile...  186 us
    slice x1, local copies, waits for them, and re-layouts, on_device(): arrived_back[0].reshape(senders * CAP, model_width)  52.7 us
  transfers between devices with their start and end apart: 4, of which 3 were waited for; matrix products, arithmetic and copies ran while one was open for 5% of the time, Pallas kernels for 0%

profile of v1, /device:TPU:27, one launch (start us, length us, event | category | flops | bytes accessed | tf_op | source)
XLA Modules:
  0.0 1065.8 jit_solution(1057188118395878668)
XLA Ops:
  7.2 0.0 copy-start
  7.2 0.9 reduce-window_1_clone.1
  8.1 0.7 subtract_bitcast_fusion
  8.7 0.8 reduce-window_clone.1
  9.6 0.7 subtract_bitcast_fusion.1
  10.2 0.1 convert_reduce_fusion
  10.3 0.7 select_reduce_fusion.2
  11.1 0.9 copy.26
  12.1 1.5 multiply_reduce_fusion.1
  13.6 0.7 fusion.48
  14.3 0.2 reduce_window_sum.27
  14.5 0.8 select_reduce_fusion
  15.3 0.7 multiply_add_fusion
  16.0 0.8 fusion.25
  16.8 1.5 fusion.3
  18.3 1.2 copy.28
  19.6 6.3 broadcast_in_dim.104
  25.9 267.1 %all_to_all.20 = bf16[2,64,18,2048]{3,0,2,1:T(2,128)(2,1)S(1)} all-to-all(bf16[2,64,18,2048]{3,0,2,1:T(2,128)(2,1)S(1)} %bitcast.73), channel_id=1, replica_groups=mesh['phase'=8,'expert'=64] {'expert'}, dimensions={1} | all-to-all | bytes 18874368 | tf_op jit(solution)/shard_map/all_to_all | solution.py:76
  293.0 52.7 %slice_reduce_fusion = (bf16[64,18,2048]{2,1,0:T(8,128)(2,1)}, bf16[64,18,2048]{2,1,0:T(8,128)(2,1)}) fusion(bf16[2,64,18,2048]{3,0,2,1:T(2,128)(2,1)S(1)} %all_to_all.20), kind=kLoop, calls=%fused_computation.1 | loop fusion | bytes 18874368 | tf_op jit(solution)/shard_map/slice | solution.py:160
  345.7 7.7 reshape_squeeze.23
  353.4 7.8 reshape_squeeze.24
  361.2 3.9 fusion.26
  365.1 0.0 copy-done.1
  365.1 0.0 copy-done.2
  365.1 1.4 fusion.35
  366.5 0.0 copy-done
  366.5 10.8 %fusion.12 = f32[1152,2048]{1,0:T(8,128)} fusion(f32[1152,128]{1,0:T(8,128)S(1)} %fusion.26, bf16[1152,2048]{1,0:T(8,128)(2,1)} %reshape_squeeze.24, f32[1152,128]{1,0:T(8,128)S(1)} %fusion.35, bf16[1,1,2048,128]{3,2,1,0:T(8,128)(2,1)S(1)} %copy-done, bf16[1,1,2048,128]{3,2,1,0:T(8,128)(2,1)S(1)} %copy-done.2), kind=kOutput, calls=%fused_computation.25 | convolution fusion | flops 1209434112 | bytes 16384000 | tf_op jit(solution)/shard_map/dot_general | solution.py:107
  377.4 7.3 fusion
  384.7 7.6 reshape.230
  392.2 9.6 all-to-all-start.3
  401.9 0.0 all-gather.4.cloned.1.call-start
  402.0 0.1 fusion.49
  402.0 0.2 reduce_window_sum.26
  402.2 0.1 select_reduce_fusion.4
  402.3 0.2 select_reduce_fusion.1
  402.5 1.5 multiply_reduce_fusion.2
  404.0 192.0 %all-to-all-done.3 = bf16[64,18,2048]{2,1,0:T(8,128)(2,1)} async-done(((bf16[64,18,2048]{2,1,0:T(8,128)(2,1)}), bf16[64,18,2048]{2,1,0:T(8,128)(2,1)}, u32[]{:S(2)}, u32[]{:S(2)}) %all-to-all-start.3) | async-done | bytes 4718624 | tf_op jit(solution)/shard_map/all_to_all | solution.py:82
  596.0 8.6 reshape.233
  604.7 5.7 reduce_sum.145
  610.3 0.0 copy-done.5
  610.3 2.5 multiply_reduce_fusion
  612.8 2.2 select_convert_fusion
  615.0 1.2 convolution_bitcast_fusion
  616.2 0.0 all-gather.4.cloned.1.call-update
  616.2 0.4 fusion.7
  616.6 2.8 broadcast_in_dim.97
  619.4 7.6 broadcast_in_dim.98
  627.0 165.6 %all_to_all.21 = bf16[1,64,18,2048]{3,2,0,1:T(8,128)(2,1)} all-to-all(bf16[1,64,18,2048]{3,2,0,1:T(8,128)(2,1)} %bitcast.74), channel_id=1, replica_groups=mesh['phase'=8,'expert'=64] {'expert'}, dimensions={1} | all-to-all | bytes 9437184 | tf_op jit(solution)/shard_map/all_to_all | solution.py:76
  792.6 7.7 reshape_squeeze.21
  800.3 3.7 fusion.37
  804.0 9.5 convolution_convert_fusion
  813.5 7.6 reshape.228
  821.1 186.3 %all_to_all.22 = bf16[64,18,2048]{2,1,0:T(8,128)(2,1)} all-to-all(bf16[64,18,2048]{2,1,0:T(8,128)(2,1)} %reshape.228), channel_id=1, replica_groups=mesh['phase'=8,'expert'=64] {'expert'}, dimensions={0} | all-to-all | bytes 9437184 | tf_op jit(solution)/shard_map/all_to_all | solution.py:82
  1007.4 8.6 reshape.231
  1016.0 5.8 reduce_sum.139
  1021.8 2.4 fusion.4
  1024.2 16.5 %collective-permute-start = (bf16[128,2048]{1,0:T(8,128)(2,1)S(1)}, bf16[128,2048]{1,0:T(8,128)(2,1)S(1)}, u32[]{:S(2)}, u32[]{:S(2)}) collective-permute-start(bf16[128,2048]{1,0:T(8,128)(2,1)S(1)} %fusion.4), channel_id=1, source_target_pairs={{0,64},{64,128},{128,192},{192,256},{256,320},{320,384},{384,448},... | collective-permute-start | bytes 1572872 | tf_op jit(solution)/shard_map/ppermute | solution.py:16
  1040.7 1.9 collective-permute-start.1
  1042.6 4.2 collective-permute-done
  1046.8 4.4 collective-permute-done.1
  1051.2 5.4 reduce_sum.147
  1056.7 0.7 copy.29
  1057.4 0.8 copy.34
  1058.2 0.8 copy.35
  (28 shorter events, 0.2 us)
Async XLA Ops:
  7.2 359.4 %copy-start = (bf16[1,1,2048,128]{3,2,1,0:T(8,128)(2,1)S(1)}, bf16[1,1,2048,128]{3,2,1,0:T(8,128)(2,1)}, u32[]{:S(2)}) copy-start(bf16[1,1,2048,128]{3,2,1,0:T(8,128)(2,1)} %param.30) | copy-start | bytes 1572868
  353.4 7.8 copy-start.3
  361.2 3.9 copy-start.1
  361.2 3.9 copy-start.2
  392.2 9.7 copy-start.6
  392.2 10.0 copy-start.9
  392.2 203.8 %all-to-all-start.3 = ((bf16[64,18,2048]{2,1,0:T(8,128)(2,1)}), bf16[64,18,2048]{2,1,0:T(8,128)(2,1)}, u32[]{:S(2)}, u32[]{:S(2)}) async-start(bf16[64,18,2048]{2,1,0:T(8,128)(2,1)} %reshape.230), calls=%async_computation.3 | async-start | bytes 12582912 | tf_op jit(solution)/shard_map/all_to_all | solution.py:82
  401.9 649.3 %all-gather.4.cloned.1.call-start = ((), (), s32[]{:S(2)}) async-start(), calls=%async_computation.4 | async-start | bytes 12779520 | tf_op jit(solution)/shard_map/all_gather | solution.py:178
  604.6 5.7 copy-start.5
  604.6 5.7 copy-start.7
  1016.0 5.8 copy-start.8
  1016.0 24.7 %copy-start.4 = (bf16[128,2048]{1,0:T(8,128)(2,1)S(1)}, bf16[128,2048]{1,0:T(8,128)(2,1)}, u32[]{:S(2)}) copy-start(bf16[128,2048]{1,0:T(8,128)(2,1)} %get-tuple-element.20) | copy-start | bytes 1572868
  1024.2 22.6 %collective-permute-start = (bf16[128,2048]{1,0:T(8,128)(2,1)S(1)}, bf16[128,2048]{1,0:T(8,128)(2,1)S(1)}, u32[]{:S(2)}, u32[]{:S(2)}) collective-permute-start(bf16[128,2048]{1,0:T(8,128)(2,1)S(1)} %fusion.4), channel_id=1, source_target_pairs={{0,64},{64,128},{128,192},{192,256},{256,320},{320,384},{384,448},... | collective-permute-start | bytes 1572872 | tf_op jit(solution)/shard_map/ppermute | solution.py:16
  1040.7 10.5 collective-permute-start.1
Sparse Core Ops, SparseCore 0:
  616.4 406.5 all-gather.3
